TPU v7x, 32 devices: a whole 2x2x4 slice. The times are simulated.
32 devices in a mesh: grp: 4 (over y, x), tp: 8 (over z, core).
Axes of the slice: x: 2, y: 2, z: 4, core: 2. Of those that a mesh axis runs over, the one named last changes fastest.
Arguments:
- batch_sizes: int32 [4], P('grp'), may hold values from 1 to 16
- seq_lens: int32 [4, 16], P('grp'), may hold values from 1 to 2048
- page_table: int32 [4, 16, 128], P('grp', None, 'tp'), may hold values from 0 to 255, as said below
- queries: bfloat16 [4, 16, 4096], P('grp', None, 'tp'), may hold values from -4 to 14
- kv_pool: bfloat16 [4, 2048, 16, 1024], P('grp', 'tp'), may hold values from -7 to 7
- new_kv: bfloat16 [4, 16, 1024], P('grp'), may hold values from -6 to 6
- out_weight: bfloat16 [4096, 2880], P('tp', 'grp'), may hold values from -0.375 to 0.375
Outputs:
- mixed: float32 [4, 16, 2880], P('grp')
Inputs may be any that keep to these rules, and one draw needn't show every extreme that they name: `batch_sizes`: slots below a group's batch size are live; the others are empty and their outputs are zero. `seq_lens`: entries of empty slots are drawn but unused. `page_table`: for every group g and every t, the entries [g, :, t * 16 to (t + 1) * 16 - 1] are a permutation of 0 to 255.
All inputs are finite; a program needn't handle non-finite values.
Results may differ from a plain program's by a relative error of at most 0.007.
Values may be sent and summed in bfloat16 or wider, within the bound.
A program may use at most 64 MiB of HBM per device.

v0:
```python
import jax
import jax.numpy as jnp
from jax import lax
from jax.sharding import PartitionSpec as P

HEADS = 64
KV_HEADS = 8
HD = 64
SLOT_BLOCK = 2


PRECISE = lax.Precision.HIGHEST
NEG_BIG = -1e30


def attend_slots(query_rows, page_blocks, lengths, tp_index, tp_count, kv_heads):
    slot_count, page_count, page_len, row_width = page_blocks.shape
    head_dim = row_width // (2 * kv_heads)
    head_count = query_rows.shape[1] // head_dim
    group_size = head_count // kv_heads
    token_count = page_count * page_len
    token_rows = page_blocks.reshape(slot_count, token_count, row_width)
    key_rows = token_rows[:, :, : row_width // 2].reshape(
        slot_count, token_count, kv_heads, head_dim
    )
    value_rows = token_rows[:, :, row_width // 2 :].reshape(
        slot_count, token_count, kv_heads, head_dim
    )
    grouped = query_rows.reshape(slot_count, kv_heads, group_size, head_dim)
    scores = jnp.einsum("skgd,stkd->skgt", grouped, key_rows, preferred_element_type=jnp.float32)
    scores = scores * head_dim ** (-0.5)
    page_index = lax.broadcasted_iota(jnp.int32, (page_count, page_len), 0)
    token_index = lax.broadcasted_iota(jnp.int32, (page_count, page_len), 1)
    position = ((page_index * tp_count + tp_index) * page_len + token_index).reshape(token_count)
    valid_mask = (position[None, :] < lengths[:, None])[:, None, None, :]
    scores = jnp.where(valid_mask, scores, NEG_BIG)
    top_score = jnp.max(scores, axis=3)
    weights = jnp.where(valid_mask, jnp.exp(scores - top_score[..., None]), 0.0)
    weight_sum = jnp.sum(weights, axis=3)
    weighted = jnp.einsum(
        "skgt,stkd->skgd",
        weights.astype(jnp.bfloat16),
        value_rows,
        preferred_element_type=jnp.float32,
    )
    return (
        weighted.reshape(slot_count, head_count * head_dim),
        top_score.reshape(slot_count, head_count),
        weight_sum.reshape(slot_count, head_count),
    )


def local(batch_sizes, seq_lens, page_table, queries, kv_pool, new_kv, out_weight):
    tp_count = lax.axis_size("tp")
    tp_index = lax.axis_index("tp")
    gathered = lax.all_gather(queries, "tp", axis=2, tiled=True)[0]
    kv_pages = kv_pool[0]
    page_ids = page_table[0]
    lengths = seq_lens[0]
    live_count = batch_sizes[0]
    slot_count, full_width = gathered.shape
    head_dim = HD
    head_count = HEADS
    slot_order = jnp.arange(slot_count, dtype=jnp.int32)

    def local_block(block_index, state):
        first_slot = block_index * SLOT_BLOCK
        query_rows = lax.dynamic_slice_in_dim(gathered, first_slot, SLOT_BLOCK, 0)
        block_ids = lax.dynamic_slice_in_dim(page_ids, first_slot, SLOT_BLOCK, 0)
        block_lengths = lax.dynamic_slice_in_dim(lengths, first_slot, SLOT_BLOCK, 0)
        block_slots = first_slot + jnp.arange(SLOT_BLOCK, dtype=jnp.int32)
        block_lengths = jnp.where(block_slots < live_count, block_lengths, 0)
        pieces = attend_slots(
            query_rows, kv_pages[block_ids], block_lengths, tp_index, tp_count, KV_HEADS
        )
        return tuple(
            (
                lax.dynamic_update_slice_in_dim(whole, piece, first_slot, 0)
                for whole, piece in zip(state, pieces)
            )
        )

    start_state = (
        jnp.zeros((slot_count, full_width), jnp.float32),
        jnp.full((slot_count, head_count), NEG_BIG, jnp.float32),
        jnp.zeros((slot_count, head_count), jnp.float32),
    )
    block_total = (live_count + SLOT_BLOCK - 1) // SLOT_BLOCK
    weighted, top_score, weight_sum = lax.fori_loop(0, block_total, local_block, start_state)
    own_heads = head_count // tp_count
    own_width = own_heads * head_dim
    shard_weighted, shard_top, shard_sum = (
        lax.all_to_all(weighted[None], "tp", split_axis=2, concat_axis=0, tiled=True),
        lax.all_to_all(top_score[None], "tp", split_axis=2, concat_axis=0, tiled=True),
        lax.all_to_all(weight_sum[None], "tp", split_axis=2, concat_axis=0, tiled=True),
    )
    part_top = jnp.max(shard_top, axis=0)
    shard_rescale = jnp.exp(shard_top - part_top[None])
    part_weighted = jnp.sum(shard_weighted * jnp.repeat(shard_rescale, head_dim, axis=-1), axis=0)
    part_sum = jnp.sum(shard_sum * shard_rescale, axis=0)
    fresh_rows = new_kv[0].astype(jnp.float32)
    kv_width = KV_HEADS * head_dim
    new_keys = fresh_rows[:, :kv_width].reshape(slot_count, KV_HEADS, head_dim)
    new_values = fresh_rows[:, kv_width:].reshape(slot_count, KV_HEADS, head_dim)
    head_ids = tp_index * own_heads + jnp.arange(own_heads, dtype=jnp.int32)
    head_map = (
        head_ids[:, None] // (head_count // KV_HEADS)
        == jnp.arange(KV_HEADS, dtype=jnp.int32)[None, :]
    ).astype(jnp.float32)
    own_keys = jnp.einsum("jk,skd->sjd", head_map, new_keys, precision=PRECISE)
    own_values = jnp.einsum("jk,skd->sjd", head_map, new_values, precision=PRECISE)
    own_queries = queries[0].astype(jnp.float32).reshape(slot_count, own_heads, head_dim)
    self_score = jnp.sum(own_queries * own_keys, axis=-1) * head_dim ** (-0.5)
    final_top = jnp.maximum(part_top, self_score)
    cache_rescale = jnp.exp(part_top - final_top)
    self_rescale = jnp.exp(self_score - final_top)
    numerator = part_weighted.reshape(slot_count, own_heads, head_dim) * cache_rescale[..., None]
    numerator = numerator + own_values * self_rescale[..., None]
    denominator = part_sum * cache_rescale + self_rescale
    attended = (numerator / denominator[..., None]).reshape(slot_count, own_width)
    attended = jnp.where((slot_order < live_count)[:, None], attended, 0.0).astype(jnp.bfloat16)
    projected = jnp.dot(
        attended,
        lax.all_gather(out_weight, "grp", axis=1, tiled=True),
        preferred_element_type=jnp.float32,
    )
    mixed = lax.psum(projected, "tp")
    return mixed[None]


def solution(mesh):
    return jax.shard_map(
        local,
        mesh=mesh,
        in_specs=(
            P("grp"),
            P("grp", None),
            P("grp", None, "tp"),
            P("grp", None, "tp"),
            P("grp", "tp", None, None),
            P("grp", None, None),
            P("tp", "grp"),
        ),
        out_specs=P("grp", None, None),
        check_vma=False,
    )
```

profile of v0, /device:TPU:0, one launch (start us, length us, event | category | flops | bytes accessed | tf_op | source)
XLA Modules:
  0.0 214.4 jit_solution(14500293375372935720)
XLA Ops:
  6.5 0.7 all-gather.2.cloned.1.call-update
  7.9 15.9 %all_gather.6 = bf16[1,16,4096]{2,1,0:T(8,128)(2,1)S(1)} all-gather(bf16[1,16,512]{2,1,0:T(8,128)(2,1)} %param.12), channel_id=1, replica_groups=mesh['grp'=4,'tp'=8] {'tp'}, dimensions={2}, use_global_device_ids=true | all-gather | bytes 147456 | tf_op jit(solution)/shard_map/all_gather | solution.py:56
  23.9 33.1 %while.14 = (s32[]{:T(128)}, f32[16,4096]{1,0:T(8,128)S(1)}, f32[16,64]{1,0:T(8,128)S(1)}, f32[16,64]{1,0:T(8,128)S(1)}, s32[]{:T(128)}, /*index=5*/s32[]{:T(128...) while((s32[]{:T(128)}, f32[16,4096]{1,0:T(8,128)S(1)}, ...), condition=%wide.region_3.4_spmd, body=%wide.region_0.3_spmd.sunk | while | flops 8685212 | bytes 7998579 | solution.py:89
  24.0 1.4 compare_select_fusion.8
  25.6 0.7 compare_select_fusion.7
  26.4 4.0 %gather_fusion = bf16[32,16,1024]{2,1,0:T(8,128)(2,1)S(1)} fusion(bf16[256,16,1024]{2,1,0:T(8,128)(2,1)} %get-tuple-element.223, s32[1024]{0:T(1024)S(1)} %pad_clamp_fusion.2), kind=kCustom, calls=%fused_computation.clone.1 | custom fusion | bytes 2097280 | tf_op jit(solution)/shard_map/while/body/gather | solution.py:74
  30.5 0.2 copy.40
  30.8 0.3 fusion.49
  31.1 0.2 fusion.51
  31.4 0.2 copy.39
  31.6 0.3 fusion.50
  32.1 1.4 compare_select_fusion.8
  33.7 0.7 compare_select_fusion.7
  34.5 4.5 %gather_fusion = bf16[32,16,1024]{2,1,0:T(8,128)(2,1)S(1)} fusion(bf16[256,16,1024]{2,1,0:T(8,128)(2,1)} %get-tuple-element.223, s32[1024]{0:T(1024)S(1)} %pad_clamp_fusion.2), kind=kCustom, calls=%fused_computation.clone.1 | custom fusion | bytes 2097280 | tf_op jit(solution)/shard_map/while/body/gather | solution.py:74
  39.1 0.2 copy.40
  39.5 0.3 fusion.49
  39.7 0.2 fusion.51
  40.1 0.2 copy.39
  40.3 0.3 fusion.50
  40.6 0.1 reshape.184
  40.8 1.4 compare_select_fusion.8
  42.4 0.7 compare_select_fusion.7
  43.2 4.0 %gather_fusion = bf16[32,16,1024]{2,1,0:T(8,128)(2,1)S(1)} fusion(bf16[256,16,1024]{2,1,0:T(8,128)(2,1)} %get-tuple-element.223, s32[1024]{0:T(1024)S(1)} %pad_clamp_fusion.2), kind=kCustom, calls=%fused_computation.clone.1 | custom fusion | bytes 2097280 | tf_op jit(solution)/shard_map/while/body/gather | solution.py:74
  47.3 0.2 copy.40
  47.6 0.3 fusion.49
  47.9 0.2 fusion.51
  48.2 0.2 copy.39
  48.4 0.3 fusion.50
  48.7 0.1 reshape.184
  48.9 1.4 compare_select_fusion.8
  50.5 0.7 compare_select_fusion.7
  51.3 4.0 %gather_fusion = bf16[32,16,1024]{2,1,0:T(8,128)(2,1)S(1)} fusion(bf16[256,16,1024]{2,1,0:T(8,128)(2,1)} %get-tuple-element.223, s32[1024]{0:T(1024)S(1)} %pad_clamp_fusion.2), kind=kCustom, calls=%fused_computation.clone.1 | custom fusion | bytes 2097280 | tf_op jit(solution)/shard_map/while/body/gather | solution.py:74
  55.4 0.2 copy.40
  55.7 0.3 fusion.49
  56.0 0.2 fusion.51
  56.4 0.2 copy.39
  56.6 0.3 fusion.50
  56.9 0.1 reshape.184
  57.1 0.5 broadcast.132
  57.6 0.7 reduce.5
  58.3 0.7 reshape.169
  59.0 4.6 %all-to-all-start.1 = ((f32[8,1,128]{2,1,0:T(1,128)}), f32[8,1,128]{2,1,0:T(1,128)S(1)}, u32[]{:S(2)}, u32[]{:S(2)}) async-start(f32[8,1,128]{2,1,0:T(1,128)} %reshape.169), calls=%async_computation.1 | async-start | bytes 8192 | tf_op jit(solution)/shard_map/all_to_all | solution.py:94
  63.8 0.7 reduce.3
  64.5 0.7 reshape.171
  65.3 3.9 %all-to-all-done.1 = f32[8,1,128]{2,1,0:T(1,128)S(1)} async-done(((f32[8,1,128]{2,1,0:T(1,128)}), f32[8,1,128]{2,1,0:T(1,128)S(1)}, u32[]{:S(2)}, u32[]{:S(2)}) %all-to-all-start.1) | async-done | bytes 4128 | tf_op jit(solution)/shard_map/all_to_all | solution.py:94
  69.2 3.3 %all-to-all-start.2 = ((f32[8,1,128]{2,1,0:T(1,128)}), f32[8,1,128]{2,1,0:T(1,128)S(1)}, u32[]{:S(2)}, u32[]{:S(2)}) async-start(f32[8,1,128]{2,1,0:T(1,128)} %reshape.171), calls=%async_computation.2 | async-start | bytes 8192 | tf_op jit(solution)/shard_map/all_to_all | solution.py:95
  72.5 0.3 fusion.14
  72.8 0.6 copy.26
  73.4 19.3 %reduce.1 = f32[4096,16]{1,0:T(8,128)} reduce(f32[4096,1,16]{2,1,0:T(1,128)S(1)} %bitcast.84, f32[]{:T(128)} %broadcast.132), dimensions={1}, to_apply=%bitcast.54.reduce_sub_computation | reduce | bytes 524292
  92.8 3.0 %reshape.167 = f32[8,1,8192]{2,1,0:T(1,128)} reshape(f32[4096,16]{1,0:T(8,128)} %reduce.1) | data formatting | bytes 524288
  95.7 5.0 %all-to-all-start = ((f32[8,1,8192]{2,1,0:T(1,128)}), f32[8,1,8192]{2,1,0:T(1,128)S(1)}, u32[]{:S(2)}, u32[]{:S(2)}) async-start(f32[8,1,8192]{2,1,0:T(1,128)} %reshape.167), calls=%async_computation | async-start | bytes 524288 | tf_op jit(solution)/shard_map/all_to_all | solution.py:93
  100.8 0.2 all-reduce.2.cloned.1.call-start
  101.2 0.6 reduce.6
  101.8 0.1 reshape.170
  101.9 0.6 reduce.4
  103.0 7.5 %all-to-all-done = f32[8,1,8192]{2,1,0:T(1,128)S(1)} async-done(((f32[8,1,8192]{2,1,0:T(1,128)}), f32[8,1,8192]{2,1,0:T(1,128)S(1)}, u32[]{:S(2)}, u32[]{:S(2)}) %all-to-all-start) | async-done | bytes 262176 | tf_op jit(solution)/shard_map/all_to_all | solution.py:93
  110.5 1.2 reduce.2
  111.7 3.9 %reshape.168 = f32[4096,1,16]{2,1,0:T(1,128)S(1)} reshape(f32[8,8192]{1,0:T(8,128)S(1)} %reduce.2) | data formatting | bytes 524288
  115.7 0.2 fusion.9
  115.9 0.1 copy.34
  116.0 0.2 fusion.13
  116.4 3.4 %convolution_bitcast_fusion = f32[1,16,2880]{2,1,0:T(8,128)} fusion(bf16[512,2880]{0,1:T(8,128)(2,1)} %all-gather.2.cloned.1.call-done, bf16[16,512]{1,0:T(8,128)(2,1)S(1)} %reshape.153, pred[16]{0:T(512)(128)(4,1)S(1)} %iota_compare_fusion.1), kind=kOutput, calls=%fused_computation.22 | convolution fusion | flops 47194112 | bytes 3149840 | tf_op jit(solution)/shard_map/dot_general | solution.py:122
  119.8 86.2 %all-reduce.2.cloned.1.call-done = f32[1,16,2880]{2,1,0:T(8,128)} async-done(((f32[1,16,2880]{2,1,0:T(8,128)}), f32[1,16,2880]{2,1,0:T(8,128)}) %all-reduce.2.cloned.1.call-update) | async-done | bytes 184336 | tf_op jit(solution)/shard_map/psum | solution.py:127
  206.0 1.6 copy.58
  (81 shorter events, 4.1 us)
Async XLA Ops:
  6.5 109.8 %all-gather.2.cloned.1.call-start = ((), (), s32[]{:S(2)}) async-start(), calls=%async_computation.3 | async-start | bytes 3686400 | tf_op jit(solution)/shard_map/all_gather | solution.py:124
  23.9 39.7 %copy-start.1 = (bf16[1,16,1024]{2,1,0:T(8,128)(2,1)S(1)}, bf16[1,16,1024]{2,1,0:T(8,128)(2,1)}, u32[]{:S(2)}) copy-start(bf16[1,16,1024]{2,1,0:T(8,128)(2,1)} %param.14) | copy-start | bytes 98308
  23.9 39.7 %copy-start = (bf16[1,16,512]{2,1,0:T(8,128)(2,1)S(1)}, bf16[1,16,512]{2,1,0:T(8,128)(2,1)}, u32[]{:S(2)}) copy-start(bf16[1,16,512]{2,1,0:T(8,128)(2,1)} %param.12) | copy-start | bytes 49156
  59.0 10.2 %all-to-all-start.1 = ((f32[8,1,128]{2,1,0:T(1,128)}), f32[8,1,128]{2,1,0:T(1,128)S(1)}, u32[]{:S(2)}, u32[]{:S(2)}) async-start(f32[8,1,128]{2,1,0:T(1,128)} %reshape.169), calls=%async_computation.1 | async-start | bytes 8192 | tf_op jit(solution)/shard_map/all_to_all | solution.py:94
  69.2 26.5 %all-to-all-start.2 = ((f32[8,1,128]{2,1,0:T(1,128)}), f32[8,1,128]{2,1,0:T(1,128)S(1)}, u32[]{:S(2)}, u32[]{:S(2)}) async-start(f32[8,1,128]{2,1,0:T(1,128)} %reshape.171), calls=%async_computation.2 | async-start | bytes 8192 | tf_op jit(solution)/shard_map/all_to_all | solution.py:95
  95.7 14.7 %all-to-all-start = ((f32[8,1,8192]{2,1,0:T(1,128)}), f32[8,1,8192]{2,1,0:T(1,128)S(1)}, u32[]{:S(2)}, u32[]{:S(2)}) async-start(f32[8,1,8192]{2,1,0:T(1,128)} %reshape.167), calls=%async_computation | async-start | bytes 524288 | tf_op jit(solution)/shard_map/all_to_all | solution.py:93
  100.8 105.2 %all-reduce.2.cloned.1.call-start = ((), (), s32[]{:S(2)}) async-start(), calls=%async_computation.4 | async-start | bytes 376832 | tf_op jit(solution)/shard_map/psum | solution.py:127
Sparse Core Ops, SparseCore 0:
  9.2 44.9 all-gather.1
  119.9 86.0 all-reduce.1
where the time goes:
time: 216 us; the launch traced here: 214 us
  waiting for transfers between devices  98.3 us (46%)
  other arithmetic  33.2 us (15%)
  local copies, waits for them, and re-layouts  33.1 us (15%)
  blocking collectives  15.9 us (7%)
  between operations  14.3 us (7%)
  starting transfers between devices  13.2 us (6%)
  matrix products  6.1 us (3%)
    psum x1, waiting for transfers between devices, local(): mixed = lax.psum(projected, 'tp')  86.2 us
    unnamed x3, other arithmetic  20.7 us
    gather x4, local copies, waits for them, and re-layouts, local_block(): kv_pages[block_ids]  16.5 us
    all_gather x1, blocking collectives, local(): gathered = lax.all_gather(queries, 'tp', axis=2, tiled=True)[0]  15.9 us
    unnamed x12, local copies, waits for them, and re-layouts  10.6 us
    all_to_all x1, waiting for transfers between devices, local(): lax.all_to_all(weighted[None], 'tp', split_axis=2, concat_axis=0, tiled=T...  7.53 us
    select_n x4, other arithmetic, local_block(): block_lengths = jnp.where(block_slots < live_count, block_lengths, 0)  5.52 us
    all_to_all x1, starting transfers between devices, local(): lax.all_to_all(weighted[None], 'tp', split_axis=2, concat_axis=0, tiled=T...  5.03 us
  transfers between devices with their start and end apart: 5, of which 3 were waited for; matrix products, arithmetic and copies ran while one was open for 31% of the time, Pallas kernels for 0%

commit v1 on v0

v1 whole, which is shorter than its diff:
```python
import functools

import jax
import jax.numpy as jnp
from jax import lax
from jax.experimental import pallas as pl
from jax.experimental.pallas import tpu as pltpu
from jax.sharding import PartitionSpec as P

HD = 64
LANES = 128
NEG_BIG = -1e30
POOL_CHUNKS = 8
MESH = pl.DeviceIdType.MESH


def fused_kernel(
    cfg,
    bs_ref,
    len_ref,
    pt_ref,
    q_hbm,
    kv_hbm,
    nkv_ref,
    w_hbm,
    out_ref,
    kv_v,
    w_v,
    q_all,
    q_bd,
    wbuf,
    w_send,
    st_send,
    w_recv,
    st_recv,
    att_all,
    ps,
    rs,
    red,
    og,
    local_sem,
    q_ssem,
    q_rsem,
    w_ssem,
    w_rsem,
    st_ssem,
    st_rsem,
    a_ssem,
    a_rsem,
    p_ssem,
    p_rsem,
    o_ssem,
    o_rsem,
):
    tp, grp, heads, kv_heads, slots, pages, page_len, cols, per, share = cfg
    t = lax.axis_index("tp")
    j = lax.axis_index("grp")
    group_size = heads // kv_heads
    own = heads // tp
    half_slots = slots // 2
    half_kv = kv_heads // 2
    tokens = pages * page_len
    key_width = kv_heads * HD
    win = key_width // 2
    owner_grp = lax.div(t, share)
    self_part = owner_grp == j

    def tp_peer(d):
        return lax.rem(t + d, tp)

    def tp_src(d):
        return lax.rem(t + (tp - d), tp)

    pool_pages = kv_v.shape[0]
    step = pool_pages // POOL_CHUNKS
    local = [
        pltpu.make_async_copy(
            kv_hbm.at[0, pl.ds(i * step, step)],
            kv_v.at[pl.ds(i * step, step)],
            local_sem.at[i],
        )
        for i in range(POOL_CHUNKS)
    ]
    w_copy = pltpu.make_async_copy(w_hbm, w_v, local_sem.at[POOL_CHUNKS])
    q_copy = pltpu.make_async_copy(q_hbm.at[0], q_all.at[t], local_sem.at[POOL_CHUNKS + 1])
    q_copy.start()
    for copy in local:
        copy.start()
    w_copy.start()

    barrier = pltpu.get_barrier_semaphore()
    for d in range(1, tp):
        pl.semaphore_signal(barrier, inc=1, device_id=(j, tp_peer(d)), device_id_type=MESH)
    for a in range(1, grp):
        pl.semaphore_signal(
            barrier, inc=1, device_id=(lax.rem(j + a, grp), t), device_id_type=MESH
        )
    for d in range(tp):
        src_t = tp_peer(d)
        if d == 0:

            @pl.when(jnp.logical_not(self_part))
            def _():
                pl.semaphore_signal(
                    barrier, inc=1, device_id=(owner_grp, src_t), device_id_type=MESH
                )

        else:
            pl.semaphore_signal(barrier, inc=1, device_id=(owner_grp, src_t), device_id_type=MESH)

    q_bd[...] = jnp.zeros_like(q_bd)
    ps[...] = jnp.zeros_like(ps)
    arrivals = (tp - 1) + (grp - 1) + grp * share
    pl.semaphore_wait(barrier, arrivals - self_part.astype(jnp.int32))

    q_sends = []
    for d in range(1, tp):
        copy = pltpu.make_async_remote_copy(
            src_ref=q_hbm.at[0],
            dst_ref=q_all.at[t],
            send_sem=q_ssem.at[d],
            recv_sem=q_rsem.at[t],
            device_id=(j, tp_peer(d)),
            device_id_type=MESH,
        )
        copy.start()
        q_sends.append(copy)
    q_copy.wait()

    lane = lax.broadcasted_iota(jnp.int32, (half_slots, LANES), 1)
    low = lane < HD

    kv_own = lax.div(t * own, group_size)
    odd = lax.rem(kv_own, 2)
    lane2 = lax.broadcasted_iota(jnp.int32, (slots, LANES), 1)
    low2 = lane2 < HD

    def kv_tile(base):
        start = pl.multiple_of(base + lax.div(kv_own, 2) * LANES, LANES)
        x = nkv_ref[0, :, pl.ds(start, LANES)].astype(jnp.float32)
        flipped = pltpu.roll(x, HD, 1)
        flip = jnp.broadcast_to(odd, x.shape) == 1
        first = jnp.where(flip, flipped, x)
        return jnp.where(low2, first, pltpu.roll(first, HD, 1))

    new_key = kv_tile(0)
    new_val = kv_tile(key_width)
    val_packed = jnp.where(low, new_val[:half_slots], new_val[half_slots:])
    q_own = q_all[t].astype(jnp.float32)
    prod = q_own * jnp.concatenate([new_key] * (own // 2), axis=1)
    prod_hi = prod.astype(jnp.bfloat16)
    prod_lo = (prod - prod_hi.astype(jnp.float32)).astype(jnp.bfloat16)
    e_row = lax.broadcasted_iota(jnp.int32, (own * HD, LANES), 0) // HD
    e_col = lax.broadcasted_iota(jnp.int32, (own * HD, LANES), 1) % own
    spread = jnp.where(e_row == e_col, 1.0, 0.0).astype(jnp.bfloat16)
    self_score = jnp.dot(prod_hi, spread, preferred_element_type=jnp.float32) + jnp.dot(
        prod_lo, spread, preferred_element_type=jnp.float32
    )
    self_score = self_score * (HD**-0.5)

    for d in range(1, tp):
        src = tp_src(d)
        pltpu.make_async_remote_copy(
            src_ref=q_hbm.at[0],
            dst_ref=q_all.at[src],
            send_sem=q_ssem.at[d],
            recv_sem=q_rsem.at[src],
            device_id=(j, src),
            device_id_type=MESH,
        ).wait_recv()
    for src in range(tp):
        rows = q_all[src].astype(jnp.float32) * (HD**-0.5)
        for pair in range(own // 2):
            tile = rows[:, pair * LANES : (pair + 1) * LANES]
            turned = pltpu.roll(tile, HD, 1)
            for side in range(2):
                head = src * own + pair * 2 + side
                kv = head // group_size
                value = tile if side == kv % 2 else turned
                keep = low2 if kv % 2 == 0 else jnp.logical_not(low2)
                value = jnp.where(keep, value, 0.0)
                q_bd[
                    (kv % half_kv) // 2, pl.ds(head, slots, stride=heads), :
                ] = value

    for copy in local:
        copy.wait()

    col = lax.broadcasted_iota(jnp.int32, (heads, tokens), 1)
    position = ((col // page_len) * tp + t) * page_len + col % page_len
    stat_lane = lax.broadcasted_iota(jnp.int32, (heads, LANES), 1)
    win_lane = lax.broadcasted_iota(jnp.int32, (group_size, win), 1) // HD
    tiles_in_win = win // LANES
    rows_in_win = half_kv * group_size

    def one_slot(s, stats):
        first = pl.multiple_of(s * heads, heads)
        ids = [pt_ref[0, s, i] for i in range(pages)]
        length = len_ref[0, s]

        def block(start):
            return jnp.concatenate(
                [kv_v[ids[i], :, start : start + win] for i in range(pages)], axis=0
            )

        scores = []
        for w in range(2):
            q_w = jnp.concatenate(
                [
                    q_bd[k, pl.ds(first + w * rows_in_win, rows_in_win), :]
                    for k in range(tiles_in_win)
                ],
                axis=1,
            ).astype(jnp.bfloat16)
            scores.append(
                lax.dot_general(
                    q_w,
                    block(w * win),
                    (((1,), (1,)), ((), ())),
                    preferred_element_type=jnp.float32,
                )
            )
        scores = jnp.concatenate(scores, axis=0)
        valid = position < length
        scores = jnp.where(valid, scores, NEG_BIG)
        top = jnp.max(scores, axis=1, keepdims=True)
        weights = jnp.where(valid, jnp.exp(scores - top), 0.0)
        total = jnp.sum(weights, axis=1, keepdims=True)
        rounded = weights.astype(jnp.bfloat16)
        tiles = []
        for w in range(2):
            o = jnp.dot(
                rounded[w * rows_in_win : (w + 1) * rows_in_win],
                block(key_width + w * win),
                preferred_element_type=jnp.float32,
            )
            folded = jnp.zeros((group_size, win), jnp.float32)
            for k in range(half_kv):
                folded = jnp.where(
                    win_lane == k, o[k * group_size : (k + 1) * group_size], folded
                )
            for k in range(tiles_in_win):
                tiles.append(folded[:, k * LANES : (k + 1) * LANES])
        stats = jnp.where(stat_lane == s, top, stats)
        stats = jnp.where(stat_lane == s + slots, total, stats)
        return tiles, stats

    g_low = lax.broadcasted_iota(jnp.int32, (group_size, LANES), 1) < HD

    def slot_pair(s, stats):
        tiles_a, stats = one_slot(s, stats)
        tiles_b, stats = one_slot(s + half_slots, stats)
        for k in range(kv_heads // 2):
            even = jnp.where(g_low, tiles_a[k], pltpu.roll(tiles_b[k], HD, 1))
            odd_t = jnp.where(g_low, pltpu.roll(tiles_a[k], HD, 1), tiles_b[k])
            span = group_size * half_slots
            wbuf[pl.ds(2 * k * span + s, group_size, stride=half_slots), :] = even
            wbuf[pl.ds((2 * k + 1) * span + s, group_size, stride=half_slots), :] = odd_t
        return stats

    stats = lax.fori_loop(0, half_slots, slot_pair, jnp.zeros((heads, LANES), jnp.float32))

    for dst in range(tp):
        span = own * half_slots
        w_send[dst] = wbuf[dst * span : (dst + 1) * span, :].astype(jnp.bfloat16)
        st_send[dst] = stats[dst * own : (dst + 1) * own]

    part_sends = []
    for d in range(1, tp):
        peer = tp_peer(d)
        for src_buf, dst_buf, ssem, rsem in (
            (st_send, st_recv, st_ssem, st_rsem),
            (w_send, w_recv, w_ssem, w_rsem),
        ):
            copy = pltpu.make_async_remote_copy(
                src_ref=src_buf.at[peer],
                dst_ref=dst_buf.at[t],
                send_sem=ssem.at[d],
                recv_sem=rsem.at[t],
                device_id=(j, peer),
                device_id_type=MESH,
            )
            copy.start()
            part_sends.append(copy)
    w_recv[t] = w_send[t]
    st_recv[t] = st_send[t]
    w_copy.wait()
    for d in range(1, tp):
        src = tp_src(d)
        pltpu.make_async_remote_copy(
            src_ref=st_send.at[src],
            dst_ref=st_recv.at[src],
            send_sem=st_ssem.at[d],
            recv_sem=st_rsem.at[src],
            device_id=(j, src),
            device_id_type=MESH,
        ).wait_recv()
    stacked = jnp.concatenate([st_recv[src] for src in range(tp)] * (LANES // heads), axis=0)
    turned = jnp.transpose(stacked)
    hs = half_slots

    def across(x, op):
        shift = own
        while shift < heads:
            x = op(x, pltpu.roll(x, shift, 1))
            shift *= 2
        return x

    parts, selfs = [], []
    for h in range(2):
        top = turned[h * hs : (h + 1) * hs]
        total = turned[slots + h * hs : slots + (h + 1) * hs]
        self_h = self_score[h * hs : (h + 1) * hs]
        final = jnp.maximum(across(top, jnp.maximum), self_h)
        scale = jnp.exp(top - final)
        self_w = jnp.exp(self_h - final)
        denominator = across(scale * total, jnp.add) + self_w
        parts.append(scale / denominator)
        selfs.append(self_w / denominator)

    def half_cast(pieces, c):
        return jnp.where(
            low,
            jnp.broadcast_to(pieces[0][:, c : c + 1], (hs, LANES)),
            jnp.broadcast_to(pieces[1][:, c : c + 1], (hs, LANES)),
        )

    sums = [half_cast(selfs, g) * val_packed for g in range(own)]
    for d in range(1, tp):
        src = tp_src(d)
        pltpu.make_async_remote_copy(
            src_ref=w_send.at[src],
            dst_ref=w_recv.at[src],
            send_sem=w_ssem.at[d],
            recv_sem=w_rsem.at[src],
            device_id=(j, src),
            device_id_type=MESH,
        ).wait_recv()
    for src in range(tp):
        block = w_recv[src].astype(jnp.float32)
        for g in range(own):
            sums[g] = sums[g] + half_cast(parts, src * own + g) * block[g * hs : (g + 1) * hs]
    tiles = []
    for k in range(own // 2):
        a, b = sums[2 * k], sums[2 * k + 1]
        upper = jnp.where(low, a, pltpu.roll(b, HD, 1))
        lower = jnp.where(low, pltpu.roll(a, HD, 1), b)
        tiles.append(jnp.concatenate([upper, lower], axis=0))
    attended = jnp.concatenate(tiles, axis=1)
    slot_row = lax.broadcasted_iota(jnp.int32, attended.shape, 0)
    attended = jnp.where(slot_row < bs_ref[0], attended, 0.0).astype(jnp.bfloat16)
    att_all[j] = attended

    a_sends = []
    for a in range(1, grp):
        copy = pltpu.make_async_remote_copy(
            src_ref=att_all.at[j],
            dst_ref=att_all.at[j],
            send_sem=a_ssem.at[a],
            recv_sem=a_rsem.at[j],
            device_id=(lax.rem(j + a, grp), t),
            device_id_type=MESH,
        )
        copy.start()
        a_sends.append(copy)
    for a in range(1, grp):
        src = lax.rem(j + (grp - a), grp)
        pltpu.make_async_remote_copy(
            src_ref=att_all.at[src],
            dst_ref=att_all.at[src],
            send_sem=a_ssem.at[a],
            recv_sem=a_rsem.at[src],
            device_id=(src, t),
            device_id_type=MESH,
        ).wait_recv()
    lhs = jnp.concatenate([att_all[g] for g in range(grp)], axis=0)
    projected = jnp.dot(lhs, w_v[...], preferred_element_type=jnp.float32)
    width = per * LANES
    for g in range(grp):
        for k in range(share):
            lo, hi = k * width, min((k + 1) * width, cols)
            if lo < hi:
                ps[g, k, :, 0 : hi - lo] = projected[g * slots : (g + 1) * slots, lo:hi].astype(
                    jnp.bfloat16
                )

    p_sends = []
    for a in range(grp):
        dst_g = lax.rem(j + a, grp)
        for k in range(share):
            dst_t = share * j + k
            copy = pltpu.make_async_remote_copy(
                src_ref=ps.at[dst_g, k],
                dst_ref=rs.at[t],
                send_sem=p_ssem.at[a, k],
                recv_sem=p_rsem.at[t],
                device_id=(dst_g, dst_t),
                device_id_type=MESH,
            )
            if a == 0:
                here = dst_t == t

                @pl.when(jnp.logical_not(here))
                def _():
                    copy.start()

                @pl.when(here)
                def _():
                    rs[t] = ps[j, k]

                p_sends.append((copy, here))
            else:
                copy.start()
                p_sends.append((copy, None))
    for d in range(tp):
        src = tp_src(d)
        copy = pltpu.make_async_remote_copy(
            src_ref=ps.at[0, 0],
            dst_ref=rs.at[src],
            send_sem=p_ssem.at[0, 0],
            recv_sem=p_rsem.at[src],
            device_id=(owner_grp, src),
            device_id_type=MESH,
        )
        if d == 0:

            @pl.when(jnp.logical_not(self_part))
            def _():
                copy.wait_recv()

        else:
            copy.wait_recv()
    total = rs[0].astype(jnp.float32)
    for src in range(1, tp):
        total = total + rs[src].astype(jnp.float32)
    red[...] = total.astype(jnp.bfloat16)

    o_sends = []
    for d in range(1, tp):
        copy = pltpu.make_async_remote_copy(
            src_ref=red,
            dst_ref=og.at[t],
            send_sem=o_ssem.at[d],
            recv_sem=o_rsem.at[t],
            device_id=(j, tp_peer(d)),
            device_id_type=MESH,
        )
        copy.start()
        o_sends.append(copy)
    og[t] = red[...]
    for copy in q_sends + part_sends + a_sends:
        copy.wait_send()
    for copy, here in p_sends:
        if here is None:
            copy.wait_send()
        else:

            @pl.when(jnp.logical_not(here))
            def _():
                copy.wait_send()

    for d in range(1, tp):
        src = tp_src(d)
        pltpu.make_async_remote_copy(
            src_ref=red,
            dst_ref=og.at[src],
            send_sem=o_ssem.at[d],
            recv_sem=o_rsem.at[src],
            device_id=(j, src),
            device_id_type=MESH,
        ).wait_recv()
    pieces = []
    for g in range(grp):
        for k in range(share):
            size = min((k + 1) * width, cols) - k * width
            if size > 0:
                pieces.append(og[g * share + k][:, :size].astype(jnp.float32))
    out_ref[0] = jnp.concatenate(pieces, axis=1)
    for copy in o_sends:
        copy.wait_send()


def local(tp, grp, batch_sizes, seq_lens, page_table, queries, kv_pool, new_kv, out_weight):
    slots, pages = page_table.shape[1:]
    pool_pages, page_len, row_width = kv_pool.shape[1:]
    kv_heads = row_width // (2 * HD)
    own_width = queries.shape[2]
    own = own_width // HD
    heads = own * tp
    rows, cols = out_weight.shape
    share = tp // grp
    tiles = -(-cols // LANES)
    per = -(-tiles // share)
    half = slots // 2
    cfg = (tp, grp, heads, kv_heads, slots, pages, page_len, cols, per, share)
    bf16, f32 = jnp.bfloat16, jnp.float32
    sem = pltpu.SemaphoreType.DMA
    vmem, smem, hbm = (
        pl.BlockSpec(memory_space=pltpu.VMEM),
        pl.BlockSpec(memory_space=pltpu.SMEM),
        pl.BlockSpec(memory_space=pl.ANY),
    )
    return pl.pallas_call(
        functools.partial(fused_kernel, cfg),
        out_shape=jax.ShapeDtypeStruct((1, slots, cols * grp), f32),
        in_specs=[smem, smem, smem, hbm, hbm, vmem, hbm],
        out_specs=vmem,
        scratch_shapes=[
            pltpu.VMEM((pool_pages, page_len, row_width), bf16),
            pltpu.VMEM((rows, cols), bf16),
            pltpu.VMEM((tp, slots, own_width), bf16),
            pltpu.VMEM((kv_heads * HD // (2 * LANES), slots * heads, LANES), f32),
            pltpu.VMEM((heads * half, LANES), f32),
            pltpu.VMEM((tp, own * half, LANES), bf16),
            pltpu.VMEM((tp, own, LANES), f32),
            pltpu.VMEM((tp, own * half, LANES), bf16),
            pltpu.VMEM((tp, own, LANES), f32),
            pltpu.VMEM((grp, slots, own_width), bf16),
            pltpu.VMEM((grp, share, slots, per * LANES), bf16),
            pltpu.VMEM((tp, slots, per * LANES), bf16),
            pltpu.VMEM((slots, per * LANES), bf16),
            pltpu.VMEM((tp, slots, per * LANES), bf16),
            sem((POOL_CHUNKS + 2,)),
            sem((tp,)),
            sem((tp,)),
            sem((tp,)),
            sem((tp,)),
            sem((tp,)),
            sem((tp,)),
            sem((grp,)),
            sem((grp,)),
            sem((grp, share)),
            sem((tp,)),
            sem((tp,)),
            sem((tp,)),
        ],
        compiler_params=pltpu.CompilerParams(
            collective_id=0, has_side_effects=True, vmem_limit_bytes=40 * 1024 * 1024
        ),
        name="fused_decode",
    )(batch_sizes, seq_lens, page_table, queries, kv_pool, new_kv, out_weight)


def solution(mesh):
    return jax.shard_map(
        functools.partial(local, mesh.shape["tp"], mesh.shape["grp"]),
        mesh=mesh,
        in_specs=(
            P("grp"),
            P("grp", None),
            P("grp", None, "tp"),
            P("grp", None, "tp"),
            P("grp", "tp", None, None),
            P("grp", None, None),
            P("tp", "grp"),
        ),
        out_specs=P("grp", None, None),
        check_vma=False,
    )
```

time: 216 us -> 48.4 us (0.22)
  waiting for transfers between devices: 98.3 us -> 0 us
  Pallas kernels: 0 us -> 39.1 us
  other arithmetic: 33.2 us -> 0 us
  local copies, waits for them, and re-layouts: 33.1 us -> 8.27 us
  blocking collectives: 15.9 us -> 0 us
  between operations: 14.3 us -> 0.68 us
  starting transfers between devices: 13.2 us -> 0 us
  matrix products: 6.1 us -> 0 us
    psum x1 -> x0, waiting for transfers between devices: 86.2 us -> none  [local(): mixed = lax.psum(projected, 'tp')]
    pallas_call x0 -> x1, Pallas kernels: none -> 39.1 us  [local(): pl.pallas_call(functools.partial(fused_kernel, cfg), out_shape=jax.ShapeD...]
    unnamed x3 -> x0, other arithmetic: 20.7 us -> none
    gather x4 -> x0, local copies, waits for them, and re-layouts: 16.5 us -> none  [local_block(): kv_pages[block_ids]]
    all_gather x1 -> x0, blocking collectives: 15.9 us -> none  [local(): gathered = lax.all_gather(queries, 'tp', axis=2, tiled=True)[0]]
    all_to_all x3 -> x0, starting transfers between devices: 12.9 us -> none  [the longest x1 5.03 us: local(): lax.all_to_all(weighted[None], 'tp', split_axis=2, concat_axis=0, tiled=T...]
    all_to_all x3 -> x0, waiting for transfers between devices: 11.4 us -> none  [the longest x1 7.53 us: local(): lax.all_to_all(weighted[None], 'tp', split_axis=2, concat_axis=0, tiled=T...]
    select_n x9 -> x0, other arithmetic: 8.32 us -> none  [the longest x4 5.52 us: local_block(): block_lengths = jnp.where(block_slots < live_count, block_lengths, 0)]
  transfers between devices with their start and end apart: 5 -> 0, of which waited for: 3 -> 0; matrix products, arithmetic and copies ran while one was open for 31% -> 0% of each run, Pallas kernels for 0% -> 0%
where the time goes in v1:
time: 48.4 us; the launch traced here: 48.1 us
  Pallas kernels  39.1 us (81%)
  local copies, waits for them, and re-layouts  8.27 us (17%)
  between operations  0.68 us (1%)
    pallas_call x1, Pallas kernels, local(): pl.pallas_call(functools.partial(fused_kernel, cfg), out_shape=jax.ShapeD...  39.1 us
    unnamed x12, local copies, waits for them, and re-layouts  8.27 us

profile of v1, /device:TPU:0, one launch (start us, length us, event | category | flops | bytes accessed | tf_op | source)
XLA Modules:
  0.0 48.1 jit_solution(553338592490352563)
XLA Ops:
  0.7 1.4 %copy.8.w_hbm = bf16[512,720]{1,0:T(8,128)(2,1)S(1)} copy(bf16[512,720]{0,1:T(8,128)(2,1)} %param.13) | data formatting | bytes 1474560 | tf_op args[6]
  2.0 0.0 copy-start
  2.1 3.4 %copy-done = bf16[1,256,16,1024]{3,2,1,0:T(8,128)(2,1)S(1)} copy-done((bf16[1,256,16,1024]{3,2,1,0:T(8,128)(2,1)S(1)}, bf16[1,256,16,1024]{3,2,1,0:T(8,128)(2,1)}, u32[]{:S(2)}) %copy-start) | copy-done | bytes 8388632
  5.4 0.0 copy-start.1
  5.4 0.8 %copy-done.1 = bf16[1,16,1024]{2,1,0:T(8,128)(2,1)S(1)} copy-done((bf16[1,16,1024]{2,1,0:T(8,128)(2,1)S(1)}, bf16[1,16,1024]{2,1,0:T(8,128)(2,1)}, u32[]{:S(2)}) %copy-start.1) | copy-done | bytes 32792
  6.2 0.0 copy-start.2
  6.2 0.7 %copy-done.2 = bf16[1,16,512]{2,1,0:T(8,128)(2,1)S(1)} copy-done((bf16[1,16,512]{2,1,0:T(8,128)(2,1)S(1)}, bf16[1,16,512]{2,1,0:T(8,128)(2,1)}, u32[]{:S(2)}) %copy-start.2) | copy-done | bytes 16408
  6.9 0.0 copy-start.3
  6.9 0.7 %copy-done.3 = s32[1,16,16]{2,1,0:T(8,128)S(1)} copy-done((s32[1,16,16]{2,1,0:T(8,128)S(1)}, s32[1,16,16]{2,1,0:T(8,128)}, u32[]{:S(2)}) %copy-start.3) | copy-done | bytes 1048
  7.6 0.0 copy-start.4
  7.6 0.7 %copy-done.4 = s32[1,16]{1,0:T(1,128)S(1)} copy-done((s32[1,16]{1,0:T(1,128)S(1)}, s32[1,16]{1,0:T(1,128)}, u32[]{:S(2)}) %copy-start.4) | copy-done | bytes 88
  8.3 39.1 %fused_decode.1 = f32[1,16,2880]{2,1,0:T(8,128)S(1)} custom-call(s32[1]{0:T(128)S(6)} %copy.10.bs_ref, s32[1,16]{1,0:T(1,128)S(1)} %copy-done.4, s32[1,16,16]{2,1,0:T(8,128)S(1)} %copy-done.3, bf16[1,16,512]{2,1,0:T(8,128)(2,1)S(1)} %copy-done.2, bf16[1,256,16,1024]{3,2,1,0:T(8,128)(2,1)S(1)} %copy-done, bf16[1,16,1024]{2,1,0:T(8,128)(2,1)S(1)} %copy-done.1, ...), custom_call_target="tpu_custom_call" | custom-call | tf_op jit(solution)/shard_map/fused_decode/pallas_call | solution.py:503
  47.4 0.7 %copy.11 = f32[1,16,2880]{2,1,0:T(8,128)} copy(f32[1,16,2880]{2,1,0:T(8,128)S(1)} %fused_decode.1) | data formatting | bytes 368640
Async XLA Ops:
  2.0 3.4 %copy-start = (bf16[1,256,16,1024]{3,2,1,0:T(8,128)(2,1)S(1)}, bf16[1,256,16,1024]{3,2,1,0:T(8,128)(2,1)}, u32[]{:S(2)}) copy-start(bf16[1,256,16,1024]{3,2,1,0:T(8,128)(2,1)} %kv_hbm.1) | copy-start | bytes 25165828
  5.4 0.8 %copy-start.1 = (bf16[1,16,1024]{2,1,0:T(8,128)(2,1)S(1)}, bf16[1,16,1024]{2,1,0:T(8,128)(2,1)}, u32[]{:S(2)}) copy-start(bf16[1,16,1024]{2,1,0:T(8,128)(2,1)} %nkv_ref.1) | copy-start | bytes 98308
  6.2 0.7 %copy-start.2 = (bf16[1,16,512]{2,1,0:T(8,128)(2,1)S(1)}, bf16[1,16,512]{2,1,0:T(8,128)(2,1)}, u32[]{:S(2)}) copy-start(bf16[1,16,512]{2,1,0:T(8,128)(2,1)} %q_hbm.1) | copy-start | bytes 49156
  6.9 0.7 %copy-start.3 = (s32[1,16,16]{2,1,0:T(8,128)S(1)}, s32[1,16,16]{2,1,0:T(8,128)}, u32[]{:S(2)}) copy-start(s32[1,16,16]{2,1,0:T(8,128)} %pt_ref.1) | copy-start | bytes 3076
  7.6 0.7 %copy-start.4 = (s32[1,16]{1,0:T(1,128)S(1)}, s32[1,16]{1,0:T(1,128)}, u32[]{:S(2)}) copy-start(s32[1,16]{1,0:T(1,128)} %len_ref.1) | copy-start | bytes 196

commit v2 on v1

--- a/solution.py
+++ b/solution.py
@@ -17,13 +17,16 @@
 def fused_kernel(
     cfg,
     bs_ref,
+    len_hbm,
+    pt_hbm,
+    q_hbm,
+    kv_hbm,
+    nkv_hbm,
+    w_hbm,
+    out_ref,
     len_ref,
     pt_ref,
-    q_hbm,
-    kv_hbm,
     nkv_ref,
-    w_hbm,
-    out_ref,
     kv_v,
     w_v,
     q_all,
@@ -83,7 +86,13 @@
     ]
     w_copy = pltpu.make_async_copy(w_hbm, w_v, local_sem.at[POOL_CHUNKS])
     q_copy = pltpu.make_async_copy(q_hbm.at[0], q_all.at[t], local_sem.at[POOL_CHUNKS + 1])
+    nkv_copy = pltpu.make_async_copy(nkv_hbm, nkv_ref, local_sem.at[POOL_CHUNKS + 2])
+    len_copy = pltpu.make_async_copy(len_hbm, len_ref, local_sem.at[POOL_CHUNKS + 3])
+    pt_copy = pltpu.make_async_copy(pt_hbm, pt_ref, local_sem.at[POOL_CHUNKS + 4])
     q_copy.start()
+    nkv_copy.start()
+    len_copy.start()
+    pt_copy.start()
     for copy in local:
         copy.start()
     w_copy.start()
@@ -95,23 +104,9 @@
         pl.semaphore_signal(
             barrier, inc=1, device_id=(lax.rem(j + a, grp), t), device_id_type=MESH
         )
-    for d in range(tp):
-        src_t = tp_peer(d)
-        if d == 0:
-
-            @pl.when(jnp.logical_not(self_part))
-            def _():
-                pl.semaphore_signal(
-                    barrier, inc=1, device_id=(owner_grp, src_t), device_id_type=MESH
-                )
-
-        else:
-            pl.semaphore_signal(barrier, inc=1, device_id=(owner_grp, src_t), device_id_type=MESH)
-
     q_bd[...] = jnp.zeros_like(q_bd)
     ps[...] = jnp.zeros_like(ps)
-    arrivals = (tp - 1) + (grp - 1) + grp * share
-    pl.semaphore_wait(barrier, arrivals - self_part.astype(jnp.int32))
+    pl.semaphore_wait(barrier, (tp - 1) + (grp - 1))
 
     q_sends = []
     for d in range(1, tp):
@@ -126,6 +121,7 @@
         copy.start()
         q_sends.append(copy)
     q_copy.wait()
+    nkv_copy.wait()
 
     lane = lax.broadcasted_iota(jnp.int32, (half_slots, LANES), 1)
     low = lane < HD
@@ -183,6 +179,8 @@
                     (kv % half_kv) // 2, pl.ds(head, slots, stride=heads), :
                 ] = value
 
+    len_copy.wait()
+    pt_copy.wait()
     for copy in local:
         copy.wait()
 
@@ -374,7 +372,9 @@
             device_id_type=MESH,
         ).wait_recv()
     lhs = jnp.concatenate([att_all[g] for g in range(grp)], axis=0)
-    projected = jnp.dot(lhs, w_v[...], preferred_element_type=jnp.float32)
+    projected = lax.dot_general(
+        lhs, w_v[...], (((1,), (1,)), ((), ())), preferred_element_type=jnp.float32
+    )
     width = per * LANES
     for g in range(grp):
         for k in range(share):
@@ -481,13 +481,14 @@
 
 
 def local(tp, grp, batch_sizes, seq_lens, page_table, queries, kv_pool, new_kv, out_weight):
+    out_weight = out_weight.T
     slots, pages = page_table.shape[1:]
     pool_pages, page_len, row_width = kv_pool.shape[1:]
     kv_heads = row_width // (2 * HD)
     own_width = queries.shape[2]
     own = own_width // HD
     heads = own * tp
-    rows, cols = out_weight.shape
+    cols, rows = out_weight.shape
     share = tp // grp
     tiles = -(-cols // LANES)
     per = -(-tiles // share)
@@ -503,11 +504,14 @@
     return pl.pallas_call(
         functools.partial(fused_kernel, cfg),
         out_shape=jax.ShapeDtypeStruct((1, slots, cols * grp), f32),
-        in_specs=[smem, smem, smem, hbm, hbm, vmem, hbm],
+        in_specs=[smem] + [hbm] * 6,
         out_specs=vmem,
         scratch_shapes=[
+            pltpu.SMEM(seq_lens.shape, jnp.int32),
+            pltpu.SMEM(page_table.shape, jnp.int32),
+            pltpu.VMEM(new_kv.shape, bf16),
             pltpu.VMEM((pool_pages, page_len, row_width), bf16),
-            pltpu.VMEM((rows, cols), bf16),
+            pltpu.VMEM((cols, rows), bf16),
             pltpu.VMEM((tp, slots, own_width), bf16),
             pltpu.VMEM((kv_heads * HD // (2 * LANES), slots * heads, LANES), f32),
             pltpu.VMEM((heads * half, LANES), f32),
@@ -520,7 +524,7 @@
             pltpu.VMEM((tp, slots, per * LANES), bf16),
             pltpu.VMEM((slots, per * LANES), bf16),
             pltpu.VMEM((tp, slots, per * LANES), bf16),
-            sem((POOL_CHUNKS + 2,)),
+            sem((POOL_CHUNKS + 5,)),
             sem((tp,)),
             sem((tp,)),
             sem((tp,)),
@@ -535,7 +539,7 @@
             sem((tp,)),
         ],
         compiler_params=pltpu.CompilerParams(
-            collective_id=0, has_side_effects=True, vmem_limit_bytes=40 * 1024 * 1024
+            collective_id=0, has_side_effects=True, vmem_limit_bytes=60 * 1024 * 1024
         ),
         name="fused_decode",
     )(batch_sizes, seq_lens, page_table, queries, kv_pool, new_kv, out_weight)

time: 48.4 us -> 41.2 us (0.85)
  local copies, waits for them, and re-layouts: 8.27 us -> 1.61 us
    unnamed x12 -> x1, local copies, waits for them, and re-layouts: 8.27 us -> 1.61 us
where the time goes in v2:
time: 41.2 us; the launch traced here: 41 us
  Pallas kernels  38.7 us (94%)
  local copies, waits for them, and re-layouts  1.61 us (4%)
  between operations  0.66 us (2%)
    pallas_call x1, Pallas kernels, local(): pl.pallas_call(functools.partial(fused_kernel, cfg), out_shape=jax.ShapeD...  38.7 us
    unnamed x1, local copies, waits for them, and re-layouts  1.61 us

profile of v2, /device:TPU:0, one launch (start us, length us, event | category | flops | bytes accessed | tf_op | source)
XLA Modules:
  0.0 41.0 jit_solution(825393753761573947)
XLA Ops:
  0.7 38.7 %fused_decode.1 = f32[1,16,2880]{2,1,0:T(8,128)} custom-call(s32[1]{0:T(128)S(6)} %copy.9.bs_ref, s32[1,16]{1,0:T(1,128)} %len_hbm.1, s32[1,16,16]{2,1,0:T(8,128)} %pt_hbm.1, bf16[1,16,512]{2,1,0:T(8,128)(2,1)} %q_hbm.1, bf16[1,256,16,1024]{3,2,1,0:T(8,128)(2,1)} %kv_hbm.1, bf16[1,16,1024]{2,1,0:T(8,128)(2,1)} %nkv_hbm.1, bf16[720,512]{1,0:T(8,128)(2,1)} %bitcast.1), custom_call_target="tpu_custom_call" | custom-call | tf_op jit(solution)/shard_map/fused_decode/pallas_call | solution.py:504
  39.4 1.6 %copy.10 = f32[1,16,2880]{2,1,0:T(8,128)} copy(f32[1,16,2880]{2,1,0:T(8,128)} %fused_decode.1) | data formatting | bytes 368640

commit v3 on v2

v3 whole, which is shorter than its diff:
```python
import functools

import jax
import jax.numpy as jnp
from jax import lax
from jax.experimental import pallas as pl
from jax.experimental.pallas import tpu as pltpu
from jax.sharding import PartitionSpec as P

HD = 64
LANES = 128
NEG_BIG = -1e30
POOL_CHUNKS = 8
MESH = pl.DeviceIdType.MESH


def fused_kernel(
    cfg,
    bs_ref,
    len_hbm,
    pt_hbm,
    q_hbm,
    kv_hbm,
    nkv_hbm,
    w_hbm,
    out_ref,
    len_ref,
    pt_ref,
    nkv_ref,
    kv_v,
    w_v,
    q_all,
    q_bd,
    wbuf,
    w_send,
    st_send,
    w_recv,
    st_recv,
    att_all,
    ps,
    rs,
    red,
    og,
    local_sem,
    q_ssem,
    q_rsem,
    w_ssem,
    w_rsem,
    st_ssem,
    st_rsem,
    a_ssem,
    a_rsem,
    p_ssem,
    p_rsem,
    o_ssem,
    o_rsem,
):
    tp, grp, heads, kv_heads, slots, pages, page_len, cols, per, share = cfg
    t = lax.axis_index("tp")
    j = lax.axis_index("grp")
    group_size = heads // kv_heads
    own = heads // tp
    half_slots = slots // 2
    half_kv = kv_heads // 2
    tokens = pages * page_len
    key_width = kv_heads * HD
    win = key_width // 2
    owner_grp = lax.div(t, share)
    self_part = owner_grp == j

    def tp_peer(d):
        return lax.rem(t + d, tp)

    def tp_src(d):
        return lax.rem(t + (tp - d), tp)

    quarter = group_size // 2

    def head_row(head):
        kv, g = head // group_size, head % group_size
        return (kv // 2) * 2 * group_size + (g % 2) * group_size + (kv % 2) * quarter + g // 2

    pool_pages = kv_v.shape[0]
    step = pool_pages // POOL_CHUNKS
    local = [
        pltpu.make_async_copy(
            kv_hbm.at[0, pl.ds(i * step, step)],
            kv_v.at[pl.ds(i * step, step)],
            local_sem.at[i],
        )
        for i in range(POOL_CHUNKS)
    ]
    w_copy = pltpu.make_async_copy(w_hbm, w_v, local_sem.at[POOL_CHUNKS])
    q_copy = pltpu.make_async_copy(q_hbm.at[0], q_all.at[t], local_sem.at[POOL_CHUNKS + 1])
    nkv_copy = pltpu.make_async_copy(nkv_hbm, nkv_ref, local_sem.at[POOL_CHUNKS + 2])
    len_copy = pltpu.make_async_copy(len_hbm, len_ref, local_sem.at[POOL_CHUNKS + 3])
    pt_copy = pltpu.make_async_copy(pt_hbm, pt_ref, local_sem.at[POOL_CHUNKS + 4])
    q_copy.start()
    nkv_copy.start()
    len_copy.start()
    pt_copy.start()
    for copy in local:
        copy.start()
    w_copy.start()

    barrier = pltpu.get_barrier_semaphore()
    for d in range(1, tp):
        pl.semaphore_signal(barrier, inc=1, device_id=(j, tp_peer(d)), device_id_type=MESH)
    for a in range(1, grp):
        pl.semaphore_signal(
            barrier, inc=1, device_id=(lax.rem(j + a, grp), t), device_id_type=MESH
        )
    q_bd[...] = jnp.zeros_like(q_bd)
    ps[...] = jnp.zeros_like(ps)
    pl.semaphore_wait(barrier, (tp - 1) + (grp - 1))

    q_sends = []
    for d in range(1, tp):
        copy = pltpu.make_async_remote_copy(
            src_ref=q_hbm.at[0],
            dst_ref=q_all.at[t],
            send_sem=q_ssem.at[d],
            recv_sem=q_rsem.at[t],
            device_id=(j, tp_peer(d)),
            device_id_type=MESH,
        )
        copy.start()
        q_sends.append(copy)
    q_copy.wait()
    nkv_copy.wait()

    lane = lax.broadcasted_iota(jnp.int32, (half_slots, LANES), 1)
    low = lane < HD

    kv_own = lax.div(t * own, group_size)
    odd = lax.rem(kv_own, 2)
    lane2 = lax.broadcasted_iota(jnp.int32, (slots, LANES), 1)
    low2 = lane2 < HD

    def kv_tile(base):
        start = pl.multiple_of(base + lax.div(kv_own, 2) * LANES, LANES)
        x = nkv_ref[0, :, pl.ds(start, LANES)].astype(jnp.float32)
        flipped = pltpu.roll(x, HD, 1)
        flip = jnp.broadcast_to(odd, x.shape) == 1
        first = jnp.where(flip, flipped, x)
        return jnp.where(low2, first, pltpu.roll(first, HD, 1))

    new_key = kv_tile(0)
    new_val = kv_tile(key_width)
    q_own = q_all[t].astype(jnp.float32)
    prod = q_own * jnp.concatenate([new_key] * (own // 2), axis=1)
    prod_hi = prod.astype(jnp.bfloat16)
    prod_lo = (prod - prod_hi.astype(jnp.float32)).astype(jnp.bfloat16)
    e_row = lax.broadcasted_iota(jnp.int32, (own * HD, LANES), 0) // HD
    e_col = lax.broadcasted_iota(jnp.int32, (own * HD, LANES), 1) % own
    e_row = (e_row % 2) * (own // 2) + e_row // 2
    spread = jnp.where(e_row == e_col, 1.0, 0.0).astype(jnp.bfloat16)
    self_score = jnp.dot(prod_hi, spread, preferred_element_type=jnp.float32) + jnp.dot(
        prod_lo, spread, preferred_element_type=jnp.float32
    )
    self_score = self_score * (HD**-0.5)

    for d in range(1, tp):
        src = tp_src(d)
        pltpu.make_async_remote_copy(
            src_ref=q_hbm.at[0],
            dst_ref=q_all.at[src],
            send_sem=q_ssem.at[d],
            recv_sem=q_rsem.at[src],
            device_id=(j, src),
            device_id_type=MESH,
        ).wait_recv()
    for src in range(tp):
        rows = q_all[src].astype(jnp.float32) * (HD**-0.5)
        for pair in range(own // 2):
            tile = rows[:, pair * LANES : (pair + 1) * LANES]
            turned = pltpu.roll(tile, HD, 1)
            for side in range(2):
                head = src * own + pair * 2 + side
                kv = head // group_size
                value = tile if side == kv % 2 else turned
                keep = low2 if kv % 2 == 0 else jnp.logical_not(low2)
                value = jnp.where(keep, value, 0.0)
                row = head_row(head)
                q_bd[(kv % half_kv) // 2, pl.ds(row, slots, stride=heads), :] = value

    len_copy.wait()
    pt_copy.wait()
    for copy in local:
        copy.wait()

    col = lax.broadcasted_iota(jnp.int32, (heads, tokens), 1)
    position = ((col // page_len) * tp + t) * page_len + col % page_len
    stat_lane = lax.broadcasted_iota(jnp.int32, (heads, LANES), 1)
    tiles_in_win = win // LANES
    rows_in_win = half_kv * group_size

    def one_slot(s):
        first = pl.multiple_of(s * heads, heads)
        ids = [pt_ref[0, s, i] for i in range(pages)]
        length = len_ref[0, s]

        def block(start):
            return jnp.concatenate(
                [kv_v[ids[i], :, start : start + win] for i in range(pages)], axis=0
            )

        scores = []
        for w in range(2):
            q_w = jnp.concatenate(
                [
                    q_bd[k, pl.ds(first + w * rows_in_win, rows_in_win), :]
                    for k in range(tiles_in_win)
                ],
                axis=1,
            ).astype(jnp.bfloat16)
            scores.append(
                lax.dot_general(
                    q_w,
                    block(w * win),
                    (((1,), (1,)), ((), ())),
                    preferred_element_type=jnp.float32,
                )
            )
        scores = jnp.concatenate(scores, axis=0)
        valid = position < length
        scores = jnp.where(valid, scores, NEG_BIG)
        top = jnp.max(scores, axis=1, keepdims=True)
        weights = jnp.where(valid, jnp.exp(scores - top), 0.0)
        total = jnp.sum(weights, axis=1, keepdims=True)
        rounded = weights.astype(jnp.bfloat16)
        tiles = []
        for w in range(2):
            o = jnp.dot(
                rounded[w * rows_in_win : (w + 1) * rows_in_win],
                block(key_width + w * win),
                preferred_element_type=jnp.float32,
            )
            for k in range(tiles_in_win):
                base = k * 2 * group_size
                lanes = slice(k * LANES, (k + 1) * LANES)
                a = o[base : base + group_size, lanes]
                b = o[base + group_size : base + 2 * group_size, lanes]
                a = jnp.where(upper, a, pltpu.roll(a, HD, 1))
                b = jnp.where(upper, pltpu.roll(b, HD, 1), b)
                tiles.append(jnp.where(g_low, a, b))
        return tiles, top, total

    g_low = lax.broadcasted_iota(jnp.int32, (group_size, LANES), 1) < HD
    upper = lax.broadcasted_iota(jnp.int32, (group_size, LANES), 0) < quarter
    hs = half_slots
    pairs = own // 2
    span = pairs * hs

    def attend_half(h):
        def body(i, stats):
            for off in (0, hs // 2):
                r = i + off
                tiles, top, total = one_slot(h * hs + r)
                for k in range(kv_heads // 2):
                    wbuf[pl.ds(k * group_size * hs + r, group_size, stride=hs), :] = tiles[k]
                stats = jnp.where(stat_lane == r, top, stats)
                stats = jnp.where(stat_lane == r + hs, total, stats)
            return stats

        stats = lax.fori_loop(0, hs // 2, body, jnp.zeros((heads, LANES), jnp.float32))
        for dst in range(tp):
            w_send[h, dst] = wbuf[dst * span : (dst + 1) * span, :].astype(jnp.bfloat16)
            for p in range(2):
                row = head_row(dst * own + p)
                st_send[h, dst, p * pairs : (p + 1) * pairs] = stats[row : row + pairs]

    def exchange(src_of, dst_buf, ssem, rsem, h):
        sends = []
        for d in range(1, tp):
            peer = tp_peer(d)
            copy = pltpu.make_async_remote_copy(
                src_ref=src_of(peer),
                dst_ref=dst_buf.at[h, t],
                send_sem=ssem.at[h, d],
                recv_sem=rsem.at[h, t],
                device_id=(j, peer),
                device_id_type=MESH,
            )
            copy.start()
            sends.append(copy)
        return sends

    def arrive(src_of, dst_buf, ssem, rsem, h):
        for d in range(1, tp):
            src = tp_src(d)
            pltpu.make_async_remote_copy(
                src_ref=src_of(src),
                dst_ref=dst_buf.at[h, src],
                send_sem=ssem.at[h, d],
                recv_sem=rsem.at[h, src],
                device_id=(j, src),
                device_id_type=MESH,
            ).wait_recv()

    def across(x, op):
        shift = own
        while shift < heads:
            x = op(x, pltpu.roll(x, shift, 1))
            shift *= 2
        return x

    def pair_cast(x, base, q):
        a, b = base + q, base + pairs + q
        return jnp.where(
            low,
            jnp.broadcast_to(x[:, a : a + 1], (hs, LANES)),
            jnp.broadcast_to(x[:, b : b + 1], (hs, LANES)),
        )

    def combine_half(h):
        arrive(lambda p: st_send.at[h, p], st_recv, st_ssem, st_rsem, h)
        stacked = jnp.concatenate(
            [st_recv[h, src] for src in range(tp)] * (LANES // heads), axis=0
        )
        turned = jnp.transpose(stacked)
        top, total = turned[:hs], turned[hs : 2 * hs]
        self_h = self_score[h * hs : (h + 1) * hs]
        final = jnp.maximum(across(top, jnp.maximum), self_h)
        scale = jnp.exp(top - final)
        self_w = jnp.exp(self_h - final)
        denominator = across(scale * total, jnp.add) + self_w
        part = scale / denominator
        own_part = self_w / denominator
        value = new_val[h * hs : (h + 1) * hs]
        sums = [pair_cast(own_part, 0, q) * value for q in range(pairs)]
        factors = [[pair_cast(part, src * own, q) for q in range(pairs)] for src in range(tp)]
        arrive(lambda p: w_send.at[h, p], w_recv, w_ssem, w_rsem, h)
        for src in range(tp):
            block = w_recv[h, src].astype(jnp.float32)
            for q in range(pairs):
                sums[q] = sums[q] + factors[src][q] * block[q * hs : (q + 1) * hs]
        attended = jnp.concatenate(sums, axis=1)
        slot_row = lax.broadcasted_iota(jnp.int32, attended.shape, 0) + h * hs
        attended = jnp.where(slot_row < bs_ref[0], attended, 0.0).astype(jnp.bfloat16)
        att_all[h, j] = attended
        sends = []
        for a in range(1, grp):
            copy = pltpu.make_async_remote_copy(
                src_ref=att_all.at[h, j],
                dst_ref=att_all.at[h, j],
                send_sem=a_ssem.at[h, a],
                recv_sem=a_rsem.at[h, j],
                device_id=(lax.rem(j + a, grp), t),
                device_id_type=MESH,
            )
            copy.start()
            sends.append(copy)
        return sends

    width = per * LANES

    def project_half(h):
        for a in range(1, grp):
            src = lax.rem(j + (grp - a), grp)
            pltpu.make_async_remote_copy(
                src_ref=att_all.at[h, src],
                dst_ref=att_all.at[h, src],
                send_sem=a_ssem.at[h, a],
                recv_sem=a_rsem.at[h, src],
                device_id=(src, t),
                device_id_type=MESH,
            ).wait_recv()
        lhs = jnp.concatenate([att_all[h, g] for g in range(grp)], axis=0)
        projected = lax.dot_general(
            lhs, w_v[...], (((1,), (1,)), ((), ())), preferred_element_type=jnp.float32
        )
        for g in range(grp):
            for k in range(share):
                lo, hi = k * width, min((k + 1) * width, cols)
                if lo < hi:
                    ps[h, g, k, :, 0 : hi - lo] = projected[
                        g * hs : (g + 1) * hs, lo:hi
                    ].astype(jnp.bfloat16)
        sends = []
        for a in range(grp):
            dst_g = lax.rem(j + a, grp)
            for k in range(share):
                dst_t = share * j + k
                copy = pltpu.make_async_remote_copy(
                    src_ref=ps.at[h, dst_g, k],
                    dst_ref=rs.at[h, t],
                    send_sem=p_ssem.at[h, a, k],
                    recv_sem=p_rsem.at[h, t],
                    device_id=(dst_g, dst_t),
                    device_id_type=MESH,
                )
                if a == 0:
                    here = dst_t == t

                    @pl.when(jnp.logical_not(here))
                    def _():
                        copy.start()

                    @pl.when(here)
                    def _():
                        rs[h, t] = ps[h, j, k]

                    sends.append((copy, here))
                else:
                    copy.start()
                    sends.append((copy, None))
        return sends

    def sum_half(h):
        for d in range(tp):
            src = tp_src(d)
            copy = pltpu.make_async_remote_copy(
                src_ref=ps.at[h, 0, 0],
                dst_ref=rs.at[h, src],
                send_sem=p_ssem.at[h, 0, 0],
                recv_sem=p_rsem.at[h, src],
                device_id=(owner_grp, src),
                device_id_type=MESH,
            )
            if d == 0:

                @pl.when(jnp.logical_not(self_part))
                def _():
                    copy.wait_recv()

            else:
                copy.wait_recv()
        total = rs[h, 0].astype(jnp.float32)
        for src in range(1, tp):
            total = total + rs[h, src].astype(jnp.float32)
        red[h] = total.astype(jnp.bfloat16)
        sends = exchange(lambda p: red.at[h], og, o_ssem, o_rsem, h)
        og[h, t] = red[h]
        return sends

    sends, p_sends = list(q_sends), []
    for h in range(2):
        attend_half(h)
        sends += exchange(lambda p: st_send.at[h, p], st_recv, st_ssem, st_rsem, h)
        sends += exchange(lambda p: w_send.at[h, p], w_recv, w_ssem, w_rsem, h)
        w_recv[h, t] = w_send[h, t]
        st_recv[h, t] = st_send[h, t]
    w_copy.wait()
    for h in range(2):
        sends += combine_half(h)
    for h in range(2):
        p_sends += project_half(h)
    for h in range(2):
        sends += sum_half(h)
    for h in range(2):
        arrive(lambda p: red.at[h], og, o_ssem, o_rsem, h)
        pieces = []
        for g in range(grp):
            for k in range(share):
                size = min((k + 1) * width, cols) - k * width
                if size > 0:
                    pieces.append(og[h, g * share + k][:, :size].astype(jnp.float32))
        out_ref[0, h * hs : (h + 1) * hs] = jnp.concatenate(pieces, axis=1)
    for copy in sends:
        copy.wait_send()
    for copy, here in p_sends:
        if here is None:
            copy.wait_send()
        else:

            @pl.when(jnp.logical_not(here))
            def _():
                copy.wait_send()


def local(tp, grp, batch_sizes, seq_lens, page_table, queries, kv_pool, new_kv, out_weight):
    out_weight = out_weight.T
    slots, pages = page_table.shape[1:]
    pool_pages, page_len, row_width = kv_pool.shape[1:]
    kv_heads = row_width // (2 * HD)
    own_width = queries.shape[2]
    own = own_width // HD
    heads = own * tp
    cols, rows = out_weight.shape
    share = tp // grp
    tiles = -(-cols // LANES)
    per = -(-tiles // share)
    half = slots // 2
    cfg = (tp, grp, heads, kv_heads, slots, pages, page_len, cols, per, share)
    bf16, f32 = jnp.bfloat16, jnp.float32
    sem = pltpu.SemaphoreType.DMA
    vmem, smem, hbm = (
        pl.BlockSpec(memory_space=pltpu.VMEM),
        pl.BlockSpec(memory_space=pltpu.SMEM),
        pl.BlockSpec(memory_space=pl.ANY),
    )
    return pl.pallas_call(
        functools.partial(fused_kernel, cfg),
        out_shape=jax.ShapeDtypeStruct((1, slots, cols * grp), f32),
        in_specs=[smem] + [hbm] * 6,
        out_specs=vmem,
        scratch_shapes=[
            pltpu.SMEM(seq_lens.shape, jnp.int32),
            pltpu.SMEM(page_table.shape, jnp.int32),
            pltpu.VMEM(new_kv.shape, bf16),
            pltpu.VMEM((pool_pages, page_len, row_width), bf16),
            pltpu.VMEM((cols, rows), bf16),
            pltpu.VMEM((tp, slots, own_width), bf16),
            pltpu.VMEM((kv_heads * HD // (2 * LANES), slots * heads, LANES), f32),
            pltpu.VMEM((heads * half // 2, LANES), f32),
            pltpu.VMEM((2, tp, own // 2 * half, LANES), bf16),
            pltpu.VMEM((2, tp, own, LANES), f32),
            pltpu.VMEM((2, tp, own // 2 * half, LANES), bf16),
            pltpu.VMEM((2, tp, own, LANES), f32),
            pltpu.VMEM((2, grp, half, own_width), bf16),
            pltpu.VMEM((2, grp, share, half, per * LANES), bf16),
            pltpu.VMEM((2, tp, half, per * LANES), bf16),
            pltpu.VMEM((2, half, per * LANES), bf16),
            pltpu.VMEM((2, tp, half, per * LANES), bf16),
            sem((POOL_CHUNKS + 5,)),
            sem((tp,)),
            sem((tp,)),
            sem((2, tp)),
            sem((2, tp)),
            sem((2, tp)),
            sem((2, tp)),
            sem((2, grp)),
            sem((2, grp)),
            sem((2, grp, share)),
            sem((2, tp)),
            sem((2, tp)),
            sem((2, tp)),
        ],
        compiler_params=pltpu.CompilerParams(
            collective_id=0, has_side_effects=True, vmem_limit_bytes=60 * 1024 * 1024
        ),
        name="fused_decode",
    )(batch_sizes, seq_lens, page_table, queries, kv_pool, new_kv, out_weight)


def solution(mesh):
    return jax.shard_map(
        functools.partial(local, mesh.shape["tp"], mesh.shape["grp"]),
        mesh=mesh,
        in_specs=(
            P("grp"),
            P("grp", None),
            P("grp", None, "tp"),
            P("grp", None, "tp"),
            P("grp", "tp", None, None),
            P("grp", None, None),
            P("tp", "grp"),
        ),
        out_specs=P("grp", None, None),
        check_vma=False,
    )
```

time: 41.2 us -> 39.3 us (0.954)
  Pallas kernels: 38.7 us -> 36.9 us
    pallas_call x1, Pallas kernels: 38.7 us -> 36.9 us  [local(): pl.pallas_call(functools.partial(fused_kernel, cfg), out_shape=jax.ShapeD...]
where the time goes in v3:
time: 39.3 us; the launch traced here: 39.1 us
  Pallas kernels  36.9 us (94%)
  local copies, waits for them, and re-layouts  1.61 us (4%)
  between operations  0.66 us (2%)
    pallas_call x1, Pallas kernels, local(): pl.pallas_call(functools.partial(fused_kernel, cfg), out_shape=jax.ShapeD...  36.9 us
    unnamed x1, local copies, waits for them, and re-layouts  1.61 us

profile of v3, /device:TPU:0, one launch (start us, length us, event | category | flops | bytes accessed | tf_op | source)
XLA Modules:
  0.0 39.1 jit_solution(16677188485130864374)
XLA Ops:
  0.7 36.9 %fused_decode.1 = f32[1,16,2880]{2,1,0:T(8,128)} custom-call(s32[1]{0:T(128)S(6)} %copy.9.bs_ref, s32[1,16]{1,0:T(1,128)} %len_hbm.1, s32[1,16,16]{2,1,0:T(8,128)} %pt_hbm.1, bf16[1,16,512]{2,1,0:T(8,128)(2,1)} %q_hbm.1, bf16[1,256,16,1024]{3,2,1,0:T(8,128)(2,1)} %kv_hbm.1, bf16[1,16,1024]{2,1,0:T(8,128)(2,1)} %nkv_hbm.1, bf16[720,512]{1,0:T(8,128)(2,1)} %bitcast.1), custom_call_target="tpu_custom_call" | custom-call | tf_op jit(solution)/shard_map/fused_decode/pallas_call | solution.py:493
  37.5 1.6 %copy.10 = f32[1,16,2880]{2,1,0:T(8,128)} copy(f32[1,16,2880]{2,1,0:T(8,128)} %fused_decode.1) | data formatting | bytes 368640

commit v4 on v3

--- a/solution.py
+++ b/solution.py
@@ -80,6 +80,14 @@
         kv, g = head // group_size, head % group_size
         return (kv // 2) * 2 * group_size + (g % 2) * group_size + (kv % 2) * quarter + g // 2
 
+    barrier = pltpu.get_barrier_semaphore()
+    for d in range(1, tp):
+        pl.semaphore_signal(barrier, inc=1, device_id=(j, tp_peer(d)), device_id_type=MESH)
+    for a in range(1, grp):
+        pl.semaphore_signal(
+            barrier, inc=1, device_id=(lax.rem(j + a, grp), t), device_id_type=MESH
+        )
+
     pool_pages = kv_v.shape[0]
     step = pool_pages // POOL_CHUNKS
     local = [
@@ -103,13 +111,6 @@
         copy.start()
     w_copy.start()
 
-    barrier = pltpu.get_barrier_semaphore()
-    for d in range(1, tp):
-        pl.semaphore_signal(barrier, inc=1, device_id=(j, tp_peer(d)), device_id_type=MESH)
-    for a in range(1, grp):
-        pl.semaphore_signal(
-            barrier, inc=1, device_id=(lax.rem(j + a, grp), t), device_id_type=MESH
-        )
     q_bd[...] = jnp.zeros_like(q_bd)
     ps[...] = jnp.zeros_like(ps)
     pl.semaphore_wait(barrier, (tp - 1) + (grp - 1))
@@ -195,8 +196,8 @@
     tiles_in_win = win // LANES
     rows_in_win = half_kv * group_size
 
-    def one_slot(s):
-        first = pl.multiple_of(s * heads, heads)
+    def slot_scores(s):
+        first = s * heads
         ids = [pt_ref[0, s, i] for i in range(pages)]
         length = len_ref[0, s]
 
@@ -222,7 +223,9 @@
                     preferred_element_type=jnp.float32,
                 )
             )
-        scores = jnp.concatenate(scores, axis=0)
+        return jnp.concatenate(scores, axis=0), block, length
+
+    def slot_values(scores, block, length):
         valid = position < length
         scores = jnp.where(valid, scores, NEG_BIG)
         top = jnp.max(scores, axis=1, keepdims=True)
@@ -253,17 +256,16 @@
     span = pairs * hs
 
     def attend_half(h):
-        def body(i, stats):
-            for off in (0, hs // 2):
-                r = i + off
-                tiles, top, total = one_slot(h * hs + r)
-                for k in range(kv_heads // 2):
-                    wbuf[pl.ds(k * group_size * hs + r, group_size, stride=hs), :] = tiles[k]
-                stats = jnp.where(stat_lane == r, top, stats)
-                stats = jnp.where(stat_lane == r + hs, total, stats)
-            return stats
-
-        stats = lax.fori_loop(0, hs // 2, body, jnp.zeros((heads, LANES), jnp.float32))
+        stats = jnp.zeros((heads, LANES), jnp.float32)
+        staged = [slot_scores(h * hs)]
+        for r in range(hs):
+            if r + 1 < hs:
+                staged.append(slot_scores(h * hs + r + 1))
+            tiles, top, total = slot_values(*staged[r])
+            for k in range(kv_heads // 2):
+                wbuf[pl.ds(k * group_size * hs + r, group_size, stride=hs), :] = tiles[k]
+            stats = jnp.where(stat_lane == r, top, stats)
+            stats = jnp.where(stat_lane == r + hs, total, stats)
         for dst in range(tp):
             w_send[h, dst] = wbuf[dst * span : (dst + 1) * span, :].astype(jnp.bfloat16)
             for p in range(2):

time: 39.3 us -> 36.3 us (0.924)
  Pallas kernels: 36.9 us -> 33.9 us
    pallas_call x1, Pallas kernels: 36.9 us -> 33.9 us  [local(): pl.pallas_call(functools.partial(fused_kernel, cfg), out_shape=jax.ShapeD...]
where the time goes in v4:
time: 36.3 us; the launch traced here: 36.2 us
  Pallas kernels  33.9 us (93%)
  local copies, waits for them, and re-layouts  1.61 us (4%)
  between operations  0.66 us (2%)
    pallas_call x1, Pallas kernels, local(): pl.pallas_call(functools.partial(fused_kernel, cfg), out_shape=jax.ShapeD...  33.9 us
    unnamed x1, local copies, waits for them, and re-layouts  1.61 us

profile of v4, /device:TPU:0, one launch (start us, length us, event | category | flops | bytes accessed | tf_op | source)
XLA Modules:
  0.0 36.2 jit_solution(14305042693366893944)
XLA Ops:
  0.7 33.9 %fused_decode.1 = f32[1,16,2880]{2,1,0:T(8,128)} custom-call(s32[1]{0:T(128)S(6)} %copy.9.bs_ref, s32[1,16]{1,0:T(1,128)} %len_hbm.1, s32[1,16,16]{2,1,0:T(8,128)} %pt_hbm.1, bf16[1,16,512]{2,1,0:T(8,128)(2,1)} %q_hbm.1, bf16[1,256,16,1024]{3,2,1,0:T(8,128)(2,1)} %kv_hbm.1, bf16[1,16,1024]{2,1,0:T(8,128)(2,1)} %nkv_hbm.1, bf16[720,512]{1,0:T(8,128)(2,1)} %bitcast.1), custom_call_target="tpu_custom_call" | custom-call | tf_op jit(solution)/shard_map/fused_decode/pallas_call | solution.py:495
  34.6 1.6 %copy.10 = f32[1,16,2880]{2,1,0:T(8,128)} copy(f32[1,16,2880]{2,1,0:T(8,128)} %fused_decode.1) | data formatting | bytes 368640

commit v5 on v4

--- a/solution.py
+++ b/solution.py
@@ -257,10 +257,11 @@
 
     def attend_half(h):
         stats = jnp.zeros((heads, LANES), jnp.float32)
-        staged = [slot_scores(h * hs)]
+        ahead = 2
+        staged = [slot_scores(h * hs + r) for r in range(ahead)]
         for r in range(hs):
-            if r + 1 < hs:
-                staged.append(slot_scores(h * hs + r + 1))
+            if r + ahead < hs:
+                staged.append(slot_scores(h * hs + r + ahead))
             tiles, top, total = slot_values(*staged[r])
             for k in range(kv_heads // 2):
                 wbuf[pl.ds(k * group_size * hs + r, group_size, stride=hs), :] = tiles[k]

time: 36.3 us -> 36 us (level)
  no operation moved by 1% of the time
where the time goes in v5:
time: 36 us; the launch traced here: 35.8 us
  Pallas kernels  33.6 us (93%)
  local copies, waits for them, and re-layouts  1.61 us (4%)
  between operations  0.66 us (2%)
    pallas_call x1, Pallas kernels, local(): pl.pallas_call(functools.partial(fused_kernel, cfg), out_shape=jax.ShapeD...  33.6 us
    unnamed x1, local copies, waits for them, and re-layouts  1.61 us

profile of v5, /device:TPU:0, one launch (start us, length us, event | category | flops | bytes accessed | tf_op | source)
XLA Modules:
  0.0 35.8 jit_solution(8554447976390262293)
XLA Ops:
  0.7 33.6 %fused_decode.1 = f32[1,16,2880]{2,1,0:T(8,128)} custom-call(s32[1]{0:T(128)S(6)} %copy.9.bs_ref, s32[1,16]{1,0:T(1,128)} %len_hbm.1, s32[1,16,16]{2,1,0:T(8,128)} %pt_hbm.1, bf16[1,16,512]{2,1,0:T(8,128)(2,1)} %q_hbm.1, bf16[1,256,16,1024]{3,2,1,0:T(8,128)(2,1)} %kv_hbm.1, bf16[1,16,1024]{2,1,0:T(8,128)(2,1)} %nkv_hbm.1, bf16[720,512]{1,0:T(8,128)(2,1)} %bitcast.1), custom_call_target="tpu_custom_call" | custom-call | tf_op jit(solution)/shard_map/fused_decode/pallas_call | solution.py:496
  34.2 1.6 %copy.10 = f32[1,16,2880]{2,1,0:T(8,128)} copy(f32[1,16,2880]{2,1,0:T(8,128)} %fused_decode.1) | data formatting | bytes 368640
